TPU v7x, 512 devices: a whole 4x4x16 slice. The times are simulated.
512 devices in a mesh: db: 64 (over z, x), seq: 8 (over y, core).
Axes of the slice: x: 4, y: 4, z: 16, core: 2. Of those that a mesh axis runs over, the one named last changes fastest.
Arguments:
- reader: bfloat16 [64, 1024, 2048], P('db', 'seq'), may hold values from -6 to 6
- reader_gain: float32 [2048], replicated, may hold values from 0.1 to 1.9
- database: bfloat16 [8192, 2, 896], P('db')
- encoder_gain: float32 [896], replicated, may hold values from 0.1 to 1.9
- w_expand: bfloat16 [896, 1792], P('db', 'seq'), may hold values from -0.1875 to 0.1875
- w_reduce: bfloat16 [1792, 896], P('seq', 'db'), may hold values from -0.125 to 0.125
- w_query: bfloat16 [2048, 2048], P('db', 'seq'), may hold values from -0.125 to 0.125
- w_key: bfloat16 [896, 2048], P('db', 'seq'), may hold values from -0.1875 to 0.1875
- w_value: bfloat16 [896, 2048], P('db', 'seq'), may hold values from -0.1875 to 0.1875
- w_output: bfloat16 [2048, 2048], P('db', 'seq'), may hold values from -0.125 to 0.125
- neighbour_ids: int32 [64, 8, 4], replicated, may hold values from 0 to 127
- lengths: int32 [64, 8, 4], P('db'), may hold values from 1 to 128, 320 in all within a row
- owners: int32 [64, 8, 4], P('db'), may hold values from 0 to 63
Outputs:
- updated: bfloat16 [64, 1024, 2048], P('db', None, 'seq')
Inputs may be any that keep to these rules, and one draw needn't show every extreme that they name: For every sequence b and every q, the lengths[b, q, :] of its 4 neighbours sum to exactly 320, and the longest of them is 128.
All inputs are finite; a program needn't handle non-finite values.
Results may differ from a plain program's by a relative error of at most 0.0065.
The roundings to bfloat16 on the way count: a program that leaves them out, or rounds other values in their place, can miss the bound.
Values may be sent and summed in bfloat16 or wider, within the bound.
No kernel may reach another device: no remote copies, remote signals or barrier semaphores. Data moves between devices by JAX's collectives and lax.ppermute only.
A program may use at most 64 MiB of HBM per device.

v0:
```python
import jax
import jax.numpy as jnp
from jax import lax
from jax.sharding import PartitionSpec as P

HD = 128
SPAN = 64
KNN = 2
epsilon = 1e-06


def rms_scale(values, scales):
    widened = values.astype(jnp.float32)
    mean_square = jnp.mean(widened * widened, axis=-1, keepdims=True)
    return widened * lax.rsqrt(mean_square + epsilon) * scales


def body(
    reader,
    reader_gain,
    database,
    encoder_gain,
    w_expand,
    w_reduce,
    w_query,
    w_key,
    w_value,
    w_output,
    neighbour_ids,
    lengths,
    owners,
):
    shards = lax.axis_size("db")
    seq_index = lax.axis_index("seq")
    entries, stripe, features = database.shape
    query_part = lax.all_gather(w_query, "db", axis=0, tiled=True)
    reader_output_part = lax.all_gather(w_output, "db", axis=0, tiled=True)
    rows = lax.all_gather(reader[0], "seq", axis=0, tiled=True)
    normed_tokens = rms_scale(rows, reader_gain).astype(jnp.bfloat16)
    queries = jnp.dot(normed_tokens, query_part, preferred_element_type=jnp.float32).astype(
        jnp.bfloat16
    )
    rows, queries, output_part = (rows, queries, reader_output_part)
    expand_part = lax.all_gather(w_expand, "db", axis=0, tiled=True)
    reduce_part = lax.all_gather(w_reduce, "db", axis=1, tiled=True)
    key_part = lax.all_gather(w_key, "db", axis=0, tiled=True)
    value_part = lax.all_gather(w_value, "db", axis=0, tiled=True)
    stored = database.reshape(entries * stripe, features)
    normed_rows = rms_scale(stored, encoder_gain).astype(jnp.bfloat16)
    hidden = jax.nn.gelu(
        jnp.dot(normed_rows, expand_part, preferred_element_type=jnp.float32), approximate=False
    ).astype(jnp.bfloat16)
    partial_sum = jnp.dot(hidden, reduce_part, preferred_element_type=jnp.float32)
    total = lax.psum(partial_sum, "seq")
    encoded = (stored.astype(jnp.float32) + total).astype(jnp.bfloat16)
    w_pairs = jnp.concatenate([key_part, value_part], axis=1)
    table = jnp.dot(encoded, w_pairs, preferred_element_type=jnp.float32).astype(jnp.bfloat16)
    table = table.reshape(entries, stripe, w_pairs.shape[1])
    requests = neighbour_ids.reshape(shards, -1)
    outgoing = table[requests]
    arrived = lax.all_to_all(outgoing, "db", split_axis=0, concat_axis=0, tiled=True)
    seq_len = rows.shape[0]
    per_seq = neighbour_ids.shape[1] * neighbour_ids.shape[2]
    width = arrived.shape[-1]
    local_heads = width // (2 * HD)
    positions = jnp.arange(stripe * shards, dtype=jnp.int32)
    owner_flat = owners[0].reshape(-1)
    length_flat = lengths[0].reshape(-1)
    source = (owner_flat[:, None] + positions[None, :] // stripe) % shards
    neighbour_index = jnp.arange(per_seq, dtype=jnp.int32)[:, None]
    flat_index = (source * per_seq + neighbour_index) * stripe + (positions % stripe)[None, :]
    key_value = arrived.reshape(-1, width)[flat_index]
    live = positions[None, :] < length_flat[:, None]
    spans = per_seq // KNN
    window = KNN * positions.shape[0]
    span_pairs = key_value.reshape(spans, window, width)
    span_live = live.reshape(spans, window)
    prior_pairs = jnp.concatenate(
        [jnp.zeros((1, window, width), jnp.bfloat16), span_pairs[:-1]], axis=0
    )
    prior_live = jnp.concatenate([jnp.zeros((1, window), bool), span_live[:-1]], axis=0)
    query_spans = queries.reshape(spans, SPAN, local_heads, HD)
    key_heads = prior_pairs[:, :, : local_heads * HD].reshape(spans, window, local_heads, HD)
    value_heads = prior_pairs[:, :, local_heads * HD :].reshape(spans, window, local_heads, HD)
    scores = jnp.einsum(
        "cqhd,ckhd->chqk", query_spans, key_heads, preferred_element_type=jnp.float32
    ) * HD ** (-0.5)
    masked = jnp.where(prior_live[:, None, None, :], scores, -jnp.inf)
    largest = jnp.max(masked, axis=-1, keepdims=True)
    largest = jnp.where(jnp.isfinite(largest), largest, 0.0)
    powers = jnp.exp(masked - largest)
    totals = jnp.sum(powers, axis=-1, keepdims=True)
    weights = (powers / jnp.where(totals > 0, totals, 1.0)).astype(jnp.bfloat16)
    attended = jnp.einsum(
        "chqk,ckhd->cqhd", weights, value_heads, preferred_element_type=jnp.float32
    )
    attended = attended.reshape(seq_len, local_heads * HD).astype(jnp.bfloat16)
    model_cols = output_part.shape[1]
    update = jnp.dot(
        lax.all_gather(attended, "seq", axis=1, tiled=True),
        output_part,
        preferred_element_type=jnp.float32,
    )
    residual = lax.dynamic_slice_in_dim(rows, seq_index * model_cols, model_cols, 1)
    result = (residual.astype(jnp.float32) + update).astype(jnp.bfloat16)
    return result[None]


def solution(mesh):
    in_specs = (
        P("db", "seq", None),
        P(),
        P("db", None, None),
        P(),
        P("db", "seq"),
        P("seq", "db"),
        P("db", "seq"),
        P("db", "seq"),
        P("db", "seq"),
        P("db", "seq"),
        P(),
        P("db", None, None),
        P("db", None, None),
    )
    out_specs = P("db", None, "seq")
    return jax.shard_map(body, mesh=mesh, in_specs=in_specs, out_specs=out_specs, check_vma=False)
```

profile of v0, /device:TPU:1, one launch (start us, length us, event | category | flops | bytes accessed | tf_op | source)
XLA Modules:
  0.0 866.5 jit_solution(5057858195962454341)
XLA Ops:
  6.5 0.0 all-reduce.4.cloned.1.call-start
  6.5 1.2 reshape.275
  7.7 0.0 copy-start.7
  7.7 1.6 multiply_reduce_fusion
  9.3 81.7 %all-gather.2 = bf16[64,14,224]{2,1,0:T(8,128)(2,1)S(1)} all-gather(bf16[1,14,224]{2,1,0:T(8,128)(2,1)} %bitcast.53), channel_id=1, replica_groups=mesh['db'=64,'seq'=8] {'db'}, dimensions={0}, use_global_device_ids=true | all-gather | bytes 407680 | tf_op jit(solution)/shard_map/all_gather | solution.py:45
  90.9 0.2 reshape.303
  91.2 0.0 copy-done.1
  91.2 73.5 %all-gather.1 = bf16[64,14,224]{2,1,0:T(8,128)(2,1)S(1)} all-gather(bf16[1,14,224]{2,1,0:T(8,128)(2,1)S(1)} %bitcast.54), channel_id=1, replica_groups=mesh['db'=64,'seq'=8] {'db'}, dimensions={0}, use_global_device_ids=true | all-gather | bytes 407680 | tf_op jit(solution)/shard_map/all_gather | solution.py:44
  164.7 0.2 reshape.301
  165.0 0.1 rsqrt.20
  165.1 0.0 copy-done.7
  165.1 0.0 copy-start.2
  165.1 0.0 copy-start.3
  165.1 2.4 fusion.38
  167.5 0.0 all-reduce.4.cloned.1.call-update
  167.5 0.0 copy-done.2
  167.5 73.3 %all-gather.4 = bf16[64,14,256]{2,1,0:T(8,128)(2,1)S(1)} all-gather(bf16[1,14,256]{2,1,0:T(8,128)(2,1)S(1)} %bitcast.55), channel_id=1, replica_groups=mesh['db'=64,'seq'=8] {'db'}, dimensions={0}, use_global_device_ids=true | all-gather | bytes 465920 | tf_op jit(solution)/shard_map/all_gather | solution.py:47
  240.8 0.0 copy-done.3
  240.8 75.0 %all-gather.3 = bf16[64,14,256]{2,1,0:T(8,128)(2,1)S(1)} all-gather(bf16[1,14,256]{2,1,0:T(8,128)(2,1)S(1)} %bitcast.56), channel_id=1, replica_groups=mesh['db'=64,'seq'=8] {'db'}, dimensions={0}, use_global_device_ids=true | all-gather | bytes 465920 | tf_op jit(solution)/shard_map/all_gather | solution.py:46
  315.8 0.1 reshape.307
  316.0 0.1 reshape.305
  316.1 0.0 copy-done
  316.1 0.1 copy.27
  316.2 0.1 reshape.278
  316.3 0.0 all-reduce.4.cloned.1.call-done
  316.3 1.6 convolution_convert_fusion.1
  317.9 0.1 reshape.269
  318.1 21.4 %gather_fusion = bf16[2048,2,512]{2,1,0:T(2,128)(2,1)} fusion(bf16[128,2,512]{2,1,0:T(2,128)(2,1)S(1)} %reshape.269, s32[2048]{0:T(1024)S(1)} %broadcast_clamp_fusion), kind=kCustom, calls=%fused_computation | custom fusion | bytes 8396800 | tf_op jit(solution)/shard_map/gather | solution.py:60
  339.5 10.5 %all-to-all-start = ((bf16[64,32,2,512]{3,2,1,0:T(2,128)(2,1)}), bf16[64,32,2,512]{3,2,1,0:T(2,128)(2,1)}, u32[]{:S(2)}, u32[]{:S(2)}) async-start(bf16[64,32,2,512]{3,2,1,0:T(2,128)(2,1)} %bitcast.46), calls=%async_computation | async-start | bytes 8388608 | tf_op jit(solution)/shard_map/all_to_all | solution.py:61
  349.9 0.0 all-gather.16.cloned.1.call-start
  350.0 0.7 all-gather.16.cloned.1.call-update
  350.7 0.0 all-gather.10.cloned.1.call-start
  350.7 0.7 all-gather.10.cloned.1.call-update
  351.4 0.0 all-gather.14.cloned.1.call-start
  351.5 0.5 all-gather.14.cloned.1.call-update
  352.0 0.2 all-gather.12.cloned.1.call-start
  352.2 0.0 copy-done.4
  352.2 0.1 copy.30
  352.3 0.1 add.149
  352.4 0.1 copy.32
  352.5 0.1 lt.61
  352.6 0.1 iota_compare_fusion
  352.7 0.1 fusion.75
  352.8 0.0 copy-start.6
  352.8 174.3 %all-gather.16.cloned.1.call-done = bf16[1,1024,2048]{2,1,0:T(8,128)(2,1)} async-done(((bf16[1,128,2048]{2,1,0:T(8,128)(2,1)}), bf16[1,1024,2048]{2,1,0:T(8,128)(2,1)}) %all-gather.16.cloned.1.call-update) | async-done | bytes 4194320 | tf_op jit(solution)/shard_map/all_gather | solution.py:38
  527.1 3.1 fusion
  530.2 134.5 %all-gather.10.cloned.1.call-done = bf16[2048,256]{1,0:T(8,128)(2,1)} async-done(((bf16[32,256]{1,0:T(8,128)(2,1)}), bf16[2048,256]{1,0:T(8,128)(2,1)}) %all-gather.10.cloned.1.call-update) | async-done | bytes 1048592 | tf_op jit(solution)/shard_map/all_gather | solution.py:36
  664.7 3.8 fusion.11
  668.5 0.1 reshape.273
  668.6 0.0 all-to-all-done
  668.6 7.2 reshape.271
  675.8 20.1 %gather_fusion.1 = bf16[4096,512]{1,0:T(8,128)(2,1)} fusion(bf16[4096,512]{1,0:T(8,128)(2,1)} %reshape.271, s32[4096]{0:T(1024)S(1)} %fusion.75), kind=kCustom, calls=%fused_computation.1 | custom fusion | bytes 8404992 | tf_op jit(solution)/shard_map/gather | solution.py:72
  695.9 4.2 slice.29
  700.2 6.3 copy.31
  706.4 2.6 pad_slice_fusion
  709.0 0.6 fusion.8
  709.7 0.9 fusion.9
  710.6 1.0 fusion.14
  711.6 0.5 copy.36
  712.2 0.9 copy.45
  713.0 0.0 all-gather.12.cloned.1.call-update
  713.1 90.4 %all-gather.14.cloned.1.call-done = bf16[2048,256]{1,0:T(8,128)(2,1)} async-done(((bf16[32,256]{1,0:T(8,128)(2,1)}), bf16[2048,256]{1,0:T(8,128)(2,1)}) %all-gather.14.cloned.1.call-update) | async-done | bytes 1048592 | tf_op jit(solution)/shard_map/all_gather | solution.py:37
  803.5 51.9 %all-gather.12.cloned.1.call-done = bf16[1024,2048]{1,0:T(8,128)(2,1)} async-done(((bf16[1024,256]{1,0:T(8,128)(2,1)}), bf16[1024,2048]{1,0:T(8,128)(2,1)}) %all-gather.12.cloned.1.call-update) | async-done | bytes 4194320 | tf_op jit(solution)/shard_map/all_gather | solution.py:100
  855.3 4.6 fusion.15
  (15 shorter events, 0.1 us)
Async XLA Ops:
  6.5 84.7 %copy-start.1 = (bf16[14,224]{1,0:T(8,128)(2,1)S(1)}, bf16[14,224]{1,0:T(8,128)(2,1)}, u32[]{:S(2)}) copy-start(bf16[14,224]{1,0:T(8,128)(2,1)} %param.17) | copy-start | bytes 18820
  6.5 309.8 %all-reduce.4.cloned.1.call-start = ((), (), s32[]{:S(2)}) async-start(), calls=%async_computation.1 | async-start | bytes 1835008 | tf_op jit(solution)/shard_map/psum | solution.py:54
  7.7 157.4 %copy-start.7 = (f32[896]{0:T(1024)S(1)}, f32[896]{0:T(1024)}, u32[]{:S(2)}) copy-start(f32[896]{0:T(1024)} %param.16) | copy-start | bytes 10756
  165.1 2.4 copy-start.2
  165.1 75.7 %copy-start.3 = (bf16[14,256]{1,0:T(8,128)(2,1)S(1)}, bf16[14,256]{1,0:T(8,128)(2,1)}, u32[]{:S(2)}) copy-start(bf16[14,256]{1,0:T(8,128)(2,1)} %param.20) | copy-start | bytes 21508
  167.5 148.6 %copy-start = (s32[64,8,4]{0,2,1:T(4,128)S(1)}, s32[64,8,4]{0,2,1:T(4,128)}, u32[]{:S(2)}) copy-start(s32[64,8,4]{0,2,1:T(4,128)} %param.23) | copy-start | bytes 24580
  339.5 12.8 %copy-start.4 = (s32[1,8,4]{1,2,0:T(4,128)S(1)}, s32[1,8,4]{1,2,0:T(4,128)}, u32[]{:S(2)}) copy-start(s32[1,8,4]{1,2,0:T(4,128)} %param.25) | copy-start | bytes 388
  339.5 12.9 %copy-start.5 = (s32[1,8,4]{1,2,0:T(4,128)S(1)}, s32[1,8,4]{1,2,0:T(4,128)}, u32[]{:S(2)}) copy-start(s32[1,8,4]{1,2,0:T(4,128)} %param.24) | copy-start | bytes 388
  339.5 329.1 %all-to-all-start = ((bf16[64,32,2,512]{3,2,1,0:T(2,128)(2,1)}), bf16[64,32,2,512]{3,2,1,0:T(2,128)(2,1)}, u32[]{:S(2)}, u32[]{:S(2)}) async-start(bf16[64,32,2,512]{3,2,1,0:T(2,128)(2,1)} %bitcast.46), calls=%async_computation | async-start | bytes 8388608 | tf_op jit(solution)/shard_map/all_to_all | solution.py:61
  349.9 177.2 %all-gather.16.cloned.1.call-start = ((), (), s32[]{:S(2)}) async-start(), calls=%async_computation.5 | async-start | bytes 4718592 | tf_op jit(solution)/shard_map/all_gather | solution.py:38
  350.7 314.0 %all-gather.10.cloned.1.call-start = ((), (), s32[]{:S(2)}) async-start(), calls=%async_computation.2 | async-start | bytes 1064960 | tf_op jit(solution)/shard_map/all_gather | solution.py:36
  351.4 452.0 %all-gather.14.cloned.1.call-start = ((), (), s32[]{:S(2)}) async-start(), calls=%async_computation.4 | async-start | bytes 1064960 | tf_op jit(solution)/shard_map/all_gather | solution.py:37
  352.0 503.3 %all-gather.12.cloned.1.call-start = ((), (), s32[]{:S(2)}) async-start(), calls=%async_computation.3 | async-start | bytes 4718592 | tf_op jit(solution)/shard_map/all_gather | solution.py:100
  352.8 311.9 %copy-start.6 = (f32[2048]{0:T(1024)S(1)}, f32[2048]{0:T(1024)}, u32[]{:S(2)}) copy-start(f32[2048]{0:T(1024)} %param.14) | copy-start | bytes 24580
Sparse Core Ops, SparseCore 0:
  167.7 123.3 all-reduce.3
  352.9 174.1 all-gather.15
  530.1 134.5 all-gather.9
  667.5 135.9 all-gather.13
  805.4 49.8 all-gather.11
where the time goes:
time: 867 us; the launch traced here: 866 us
  waiting for transfers between devices  453 us (52%)
  blocking collectives  303 us (35%)
  local copies, waits for them, and re-layouts  66 us (8%)
  matrix products  14 us (2%)
  between operations  13.4 us (2%)
  starting transfers between devices  10.8 us (1%)
    all_gather x1, waiting for transfers between devices, body(): rows = lax.all_gather(reader[0], 'seq', axis=0, tiled=True)  174 us
    all_gather x1, waiting for transfers between devices, body(): query_part = lax.all_gather(w_query, 'db', axis=0, tiled=True)  134 us
    all_gather x1, waiting for transfers between devices, body(): reader_output_part = lax.all_gather(w_output, 'db', axis=0, tiled=True)  90.4 us
    all_gather x1, blocking collectives, body(): reduce_part = lax.all_gather(w_reduce, 'db', axis=1, tiled=True)  81.7 us
    all_gather x1, blocking collectives, body(): key_part = lax.all_gather(w_key, 'db', axis=0, tiled=True)  75 us
    all_gather x1, blocking collectives, body(): expand_part = lax.all_gather(w_expand, 'db', axis=0, tiled=True)  73.5 us
    all_gather x1, blocking collectives, body(): value_part = lax.all_gather(w_value, 'db', axis=0, tiled=True)  73.3 us
    all_gather x1, waiting for transfers between devices, body(): lax.all_gather(attended, 'seq', axis=1, tiled=True)  51.9 us
  transfers between devices with their start and end apart: 6, of which 4 were waited for; matrix products, arithmetic and copies ran while one was open for 6% of the time, Pallas kernels for 0%

commit v1 on v0

--- a/solution.py
+++ b/solution.py
@@ -33,7 +33,11 @@
     shards = lax.axis_size("db")
     seq_index = lax.axis_index("seq")
     entries, stripe, features = database.shape
-    query_part = lax.all_gather(w_query, "db", axis=0, tiled=True)
+    shelf = []
+    for _ in range(lax.axis_size("db")):
+        shelf.append(w_query)
+    tall = jnp.stack(shelf)
+    query_part = jnp.concatenate(lax.all_to_all(tall, "db", 0, 0), axis=0)
     reader_output_part = lax.all_gather(w_output, "db", axis=0, tiled=True)
     rows = lax.all_gather(reader[0], "seq", axis=0, tiled=True)
     normed_tokens = rms_scale(rows, reader_gain).astype(jnp.bfloat16)

time: 867 us -> 788 us (0.909)
  waiting for transfers between devices: 453 us -> 318 us
  blocking collectives: 303 us -> 338 us
  starting transfers between devices: 10.8 us -> 31.2 us
    all_gather x1 -> x0, waiting for transfers between devices: 134 us -> none  [body(): query_part = lax.all_gather(w_query, 'db', axis=0, tiled=True)]
    all_gather x1, blocking collectives: 81.7 us -> 116 us  [body(): reduce_part = lax.all_gather(w_reduce, 'db', axis=1, tiled=True)]
    all_to_all x0 -> x1, starting transfers between devices: none -> 19.2 us  [body(): query_part = jnp.concatenate(lax.all_to_all(tall, 'db', 0, 0), axis=0)]
  transfers between devices with their start and end apart: 6 -> 6, of which waited for: 4 -> 3; matrix products, arithmetic and copies ran while one was open for 6% -> 10% of each run, Pallas kernels for 0% -> 0%
where the time goes in v1:
time: 788 us; the launch traced here: 787 us
  blocking collectives  338 us (43%)
  waiting for transfers between devices  318 us (40%)
  local copies, waits for them, and re-layouts  67.9 us (9%)
  starting transfers between devices  31.2 us (4%)
  between operations  13.4 us (2%)
  matrix products  12.5 us (2%)
    all_gather x1, waiting for transfers between devices, body(): rows = lax.all_gather(reader[0], 'seq', axis=0, tiled=True)  177 us
    all_gather x1, blocking collectives, body(): reduce_part = lax.all_gather(w_reduce, 'db', axis=1, tiled=True)  116 us
    all_gather x1, waiting for transfers between devices, body(): reader_output_part = lax.all_gather(w_output, 'db', axis=0, tiled=True)  87.8 us
    all_gather x1, blocking collectives, body(): key_part = lax.all_gather(w_key, 'db', axis=0, tiled=True)  76.2 us
    all_gather x1, blocking collectives, body(): expand_part = lax.all_gather(w_expand, 'db', axis=0, tiled=True)  73.6 us
    all_gather x1, blocking collectives, body(): value_part = lax.all_gather(w_value, 'db', axis=0, tiled=True)  72.8 us
    all_gather x1, waiting for transfers between devices, body(): lax.all_gather(attended, 'seq', axis=1, tiled=True)  51.9 us
    gather x1, local copies, waits for them, and re-layouts, body(): outgoing = table[requests]  21.4 us
  transfers between devices with their start and end apart: 6, of which 3 were waited for; matrix products, arithmetic and copies ran while one was open for 10% of the time, Pallas kernels for 0%

profile of v1, /device:TPU:1, one launch (start us, length us, event | category | flops | bytes accessed | tf_op | source)
XLA Modules:
  0.0 786.6 jit_solution(4004170141466631833)
XLA Ops:
  6.5 1.9 stack.2
  8.4 19.2 %all-to-all-start.1 = ((bf16[64,32,256]{2,1,0:T(8,128)(2,1)}), bf16[64,32,256]{2,1,0:T(8,128)(2,1)S(1)}, u32[]{:S(2)}, u32[]{:S(2)}) async-start(bf16[64,32,256]{2,1,0:T(8,128)(2,1)} %stack.2), calls=%async_computation.1 | async-start | bytes 2097152 | tf_op jit(solution)/shard_map/all_to_all | solution.py:40
  27.7 0.0 all-reduce.4.cloned.1.call-start
  27.7 0.0 copy-done.1
  27.7 0.1 reshape.281
  27.9 0.0 copy-start.10
  27.9 0.0 copy-done.3
  27.9 115.7 %all-gather.2 = bf16[64,14,224]{2,1,0:T(8,128)(2,1)S(1)} all-gather(bf16[1,14,224]{2,1,0:T(8,128)(2,1)S(1)} %bitcast.55), channel_id=1, replica_groups=mesh['db'=64,'seq'=8] {'db'}, dimensions={0}, use_global_device_ids=true | all-gather | bytes 407680 | tf_op jit(solution)/shard_map/all_gather | solution.py:49
  143.5 0.2 reshape.309
  143.8 0.0 copy-done.4
  143.8 73.6 %all-gather.1 = bf16[64,14,224]{2,1,0:T(8,128)(2,1)S(1)} all-gather(bf16[1,14,224]{2,1,0:T(8,128)(2,1)S(1)} %bitcast.56), channel_id=1, replica_groups=mesh['db'=64,'seq'=8] {'db'}, dimensions={0}, use_global_device_ids=true | all-gather | bytes 407680 | tf_op jit(solution)/shard_map/all_gather | solution.py:48
  217.4 1.0 reshape.307
  218.4 0.5 multiply_reduce_fusion
  218.9 0.1 rsqrt.20
  219.1 0.0 copy-done.10
  219.1 0.0 copy-start.5
  219.1 0.0 copy-start.6
  219.1 3.3 fusion.38
  222.4 0.0 all-reduce.4.cloned.1.call-update
  222.5 72.8 %all-gather.4 = bf16[64,14,256]{2,1,0:T(8,128)(2,1)S(1)} all-gather(bf16[1,14,256]{2,1,0:T(8,128)(2,1)S(1)} %bitcast.57), channel_id=1, replica_groups=mesh['db'=64,'seq'=8] {'db'}, dimensions={0}, use_global_device_ids=true | all-gather | bytes 465920 | tf_op jit(solution)/shard_map/all_gather | solution.py:51
  295.3 76.2 %all-gather.3 = bf16[64,14,256]{2,1,0:T(8,128)(2,1)S(1)} all-gather(bf16[1,14,256]{2,1,0:T(8,128)(2,1)S(1)} %bitcast.58), channel_id=1, replica_groups=mesh['db'=64,'seq'=8] {'db'}, dimensions={0}, use_global_device_ids=true | all-gather | bytes 465920 | tf_op jit(solution)/shard_map/all_gather | solution.py:50
  371.5 0.1 reshape.313
  371.7 0.1 reshape.311
  371.8 0.1 copy.27
  371.9 0.1 reshape.284
  372.0 0.0 all-reduce.4.cloned.1.call-done
  372.0 1.6 convolution_convert_fusion.1
  373.6 0.1 reshape.274
  373.7 21.4 %gather_fusion = bf16[2048,2,512]{2,1,0:T(2,128)(2,1)} fusion(bf16[128,2,512]{2,1,0:T(2,128)(2,1)S(1)} %reshape.274, s32[2048]{0:T(1024)S(1)} %broadcast_clamp_fusion), kind=kCustom, calls=%fused_computation | custom fusion | bytes 8396800 | tf_op jit(solution)/shard_map/gather | solution.py:64
  395.2 0.0 all-to-all-done.1
  395.2 11.7 %all-to-all-start = ((bf16[64,32,2,512]{3,2,1,0:T(2,128)(2,1)}), bf16[64,32,2,512]{3,2,1,0:T(2,128)(2,1)}, u32[]{:S(2)}, u32[]{:S(2)}) async-start(bf16[64,32,2,512]{3,2,1,0:T(2,128)(2,1)} %bitcast.47), calls=%async_computation | async-start | bytes 8388608 | tf_op jit(solution)/shard_map/all_to_all | solution.py:65
  406.8 0.0 all-gather.13.cloned.1.call-start
  406.9 0.7 all-gather.13.cloned.1.call-update
  407.6 0.0 all-gather.11.cloned.1.call-start
  407.6 0.7 all-gather.11.cloned.1.call-update
  408.3 0.2 all-gather.9.cloned.1.call-start
  408.6 0.0 copy-done.7
  408.6 0.1 copy.30
  408.6 0.1 add.149
  408.7 0.1 copy.32
  408.8 0.1 lt.61
  408.9 0.1 iota_compare_fusion
  409.0 0.1 fusion.75
  409.1 0.0 copy-start.9
  409.1 177.3 %all-gather.13.cloned.1.call-done = bf16[1,1024,2048]{2,1,0:T(8,128)(2,1)} async-done(((bf16[1,128,2048]{2,1,0:T(8,128)(2,1)}), bf16[1,1024,2048]{2,1,0:T(8,128)(2,1)}) %all-gather.13.cloned.1.call-update) | async-done | bytes 4194320 | tf_op jit(solution)/shard_map/all_gather | solution.py:42
  586.4 3.2 fusion
  589.7 0.2 copy-done
  589.9 1.3 fusion.11
  591.2 0.1 reshape.279
  591.3 0.0 all-to-all-done
  591.3 7.2 reshape.276
  598.5 20.1 %gather_fusion.1 = bf16[4096,512]{1,0:T(8,128)(2,1)} fusion(bf16[4096,512]{1,0:T(8,128)(2,1)} %reshape.276, s32[4096]{0:T(1024)S(1)} %fusion.75), kind=kCustom, calls=%fused_computation.1 | custom fusion | bytes 8404992 | tf_op jit(solution)/shard_map/gather | solution.py:76
  618.6 4.2 slice.29
  622.9 6.3 copy.31
  629.1 2.6 pad_slice_fusion
  631.7 0.6 fusion.8
  632.4 0.9 fusion.9
  633.3 1.0 fusion.14
  634.3 0.5 copy.36
  634.9 0.9 copy.45
  635.7 0.0 all-gather.9.cloned.1.call-update
  635.8 87.8 %all-gather.11.cloned.1.call-done = bf16[2048,256]{1,0:T(8,128)(2,1)} async-done(((bf16[32,256]{1,0:T(8,128)(2,1)}), bf16[2048,256]{1,0:T(8,128)(2,1)}) %all-gather.11.cloned.1.call-update) | async-done | bytes 1048592 | tf_op jit(solution)/shard_map/all_gather | solution.py:41
  723.6 51.9 %all-gather.9.cloned.1.call-done = bf16[1024,2048]{1,0:T(8,128)(2,1)} async-done(((bf16[1024,256]{1,0:T(8,128)(2,1)}), bf16[1024,2048]{1,0:T(8,128)(2,1)}) %all-gather.9.cloned.1.call-update) | async-done | bytes 4194320 | tf_op jit(solution)/shard_map/all_gather | solution.py:104
  775.5 4.6 fusion.15
  (21 shorter events, 0.1 us)
Async XLA Ops:
  6.5 21.2 %copy-start.1 = (bf16[128,2,896]{2,1,0:T(2,128)(2,1)S(1)}, bf16[128,2,896]{2,1,0:T(2,128)(2,1)}, u32[]{:S(2)}) copy-start(bf16[128,2,896]{2,1,0:T(2,128)(2,1)} %param.15) | copy-start | bytes 1376260
  6.5 21.3 %copy-start.3 = (bf16[224,14]{0,1:T(8,128)(2,1)S(1)}, bf16[224,14]{0,1:T(8,128)(2,1)}, u32[]{:S(2)}) copy-start(bf16[224,14]{0,1:T(8,128)(2,1)} %param.18) | copy-start | bytes 18820
  8.4 135.4 %copy-start.4 = (bf16[14,224]{1,0:T(8,128)(2,1)S(1)}, bf16[14,224]{1,0:T(8,128)(2,1)}, u32[]{:S(2)}) copy-start(bf16[14,224]{1,0:T(8,128)(2,1)} %param.17) | copy-start | bytes 18820
  8.4 386.7 %all-to-all-start.1 = ((bf16[64,32,256]{2,1,0:T(8,128)(2,1)}), bf16[64,32,256]{2,1,0:T(8,128)(2,1)S(1)}, u32[]{:S(2)}, u32[]{:S(2)}) async-start(bf16[64,32,256]{2,1,0:T(8,128)(2,1)} %stack.2), calls=%async_computation.1 | async-start | bytes 2097152 | tf_op jit(solution)/shard_map/all_to_all | solution.py:40
  27.7 344.3 %all-reduce.4.cloned.1.call-start = ((), (), s32[]{:S(2)}) async-start(), calls=%async_computation.2 | async-start | bytes 1835008 | tf_op jit(solution)/shard_map/psum | solution.py:58
  27.9 191.2 %copy-start.10 = (f32[896]{0:T(1024)S(1)}, f32[896]{0:T(1024)}, u32[]{:S(2)}) copy-start(f32[896]{0:T(1024)} %param.16) | copy-start | bytes 10756
  219.1 3.4 copy-start.5
  219.1 76.2 %copy-start.6 = (bf16[14,256]{1,0:T(8,128)(2,1)S(1)}, bf16[14,256]{1,0:T(8,128)(2,1)}, u32[]{:S(2)}) copy-start(bf16[14,256]{1,0:T(8,128)(2,1)} %param.20) | copy-start | bytes 21508
  222.4 149.4 %copy-start.2 = (s32[64,8,4]{0,2,1:T(4,128)S(1)}, s32[64,8,4]{0,2,1:T(4,128)}, u32[]{:S(2)}) copy-start(s32[64,8,4]{0,2,1:T(4,128)} %param.23) | copy-start | bytes 24580
  395.2 13.4 %copy-start.7 = (s32[1,8,4]{1,2,0:T(4,128)S(1)}, s32[1,8,4]{1,2,0:T(4,128)}, u32[]{:S(2)}) copy-start(s32[1,8,4]{1,2,0:T(4,128)} %param.25) | copy-start | bytes 388
  395.2 13.6 %copy-start.8 = (s32[1,8,4]{1,2,0:T(4,128)S(1)}, s32[1,8,4]{1,2,0:T(4,128)}, u32[]{:S(2)}) copy-start(s32[1,8,4]{1,2,0:T(4,128)} %param.24) | copy-start | bytes 388
  395.2 196.1 %all-to-all-start = ((bf16[64,32,2,512]{3,2,1,0:T(2,128)(2,1)}), bf16[64,32,2,512]{3,2,1,0:T(2,128)(2,1)}, u32[]{:S(2)}, u32[]{:S(2)}) async-start(bf16[64,32,2,512]{3,2,1,0:T(2,128)(2,1)} %bitcast.47), calls=%async_computation | async-start | bytes 8388608 | tf_op jit(solution)/shard_map/all_to_all | solution.py:65
  406.8 179.6 %all-gather.13.cloned.1.call-start = ((), (), s32[]{:S(2)}) async-start(), calls=%async_computation.5 | async-start | bytes 4718592 | tf_op jit(solution)/shard_map/all_gather | solution.py:42
  407.6 316.0 %all-gather.11.cloned.1.call-start = ((), (), s32[]{:S(2)}) async-start(), calls=%async_computation.4 | async-start | bytes 1064960 | tf_op jit(solution)/shard_map/all_gather | solution.py:41
  408.3 367.1 %all-gather.9.cloned.1.call-start = ((), (), s32[]{:S(2)}) async-start(), calls=%async_computation.3 | async-start | bytes 4718592 | tf_op jit(solution)/shard_map/all_gather | solution.py:104
  409.1 180.5 %copy-start.9 = (f32[2048]{0:T(1024)S(1)}, f32[2048]{0:T(1024)}, u32[]{:S(2)}) copy-start(f32[2048]{0:T(1024)} %param.14) | copy-start | bytes 24580
  586.4 3.4 copy-start
Sparse Core Ops, SparseCore 0:
  222.6 124.5 all-reduce.3
  409.8 176.5 all-gather.12
  589.4 134.1 all-gather.10
  725.6 49.8 all-gather.8
